TPU v7x, 32 devices: a whole 2x2x4 slice. The times are simulated.
32 devices in a mesh: comp: 4 (over y, core), tile: 8 (over z, x).
Axes of the slice: x: 2, y: 2, z: 4, core: 2. Of those that a mesh axis runs over, the one named last changes fastest.
Arguments:
- column_state: float32 [4, 8, 4, 16, 2048], P('comp', 'tile'), may hold values from -6 to 6
- mixing: float32 [2, 4, 16], replicated, may hold values from 0.02 to 0.24
- vertical: float32 [2, 16, 16], replicated, may hold values from -1.5 to 1.5
- flux_coef: float32 [2, 4], replicated, may hold values from 0.5 to 1.5
- atm_block: int32 [4, 8, 16], P('comp', 'tile'), may hold values from 0 to 15
- ocean_block: int32 [4, 8, 16], P('comp', 'tile'), may hold values from 0 to 15
- tile_offset: int32 [4, 8, 16], P('comp', 'tile'), may hold values from 0 to 6
- remap_weights: bfloat16 [4, 8, 16, 128, 128], P('comp', 'tile'), may hold values from 0 to 0.119628906
- ocean_mask: int32 [8, 2048], P('tile'), may hold values 0 or 1
Outputs:
- new_state: float32 [4, 8, 4, 16, 2048], P('comp', 'tile')
Inputs may be any that keep to these rules, and one draw needn't show every extreme that they name: `atm_block`: entries at comp index 3 are not read.
All inputs are finite; a program needn't handle non-finite values. No bound on the sum of `ocean_mask` on one device may be relied on, other than what follows from the above.
Results may differ from a plain program's by a relative error of at most 0.0003.
Values sent between devices are 32-bit elements; how exact they have to be, the bound alone decides.
No kernel may reach another device: no remote copies, remote signals or barrier semaphores. Data moves between devices by JAX's collectives and lax.ppermute only.
A program may use at most 64 MiB of HBM per device.

v0:
```python
import jax
import jax.numpy as jnp
from jax import lax
from jax.sharding import PartitionSpec as P

REACH = 3
SUB = 2


def extended(cells, sides, width):
    for axis, dim in sides:
        count = lax.axis_size(axis)
        head = lax.slice_in_dim(cells, 0, width, axis=dim)
        tail = lax.slice_in_dim(cells, cells.shape[dim] - width, cells.shape[dim], axis=dim)
        cells = jnp.concatenate(
            [
                lax.ppermute(tail, axis, [(i, (i + 1) % count) for i in range(count)]),
                cells,
                lax.ppermute(head, axis, [((i + 1) % count, i) for i in range(count)]),
            ],
            axis=dim,
        )
    return cells


def passed_along(value, axis, steps):
    count = lax.axis_size(axis)
    pairs = [(source, (source + steps) % count) for source in range(count)]
    return lax.ppermute(value, axis, pairs)


def local(
    column_state,
    mixing,
    vertical,
    flux_coef,
    atm_block,
    ocean_block,
    tile_offset,
    remap_weights,
    ocean_mask,
):
    fields = column_state[0, 0]
    cells = fields.shape[2]
    across = remap_weights.shape[3]
    ocean_cells = remap_weights.shape[4]
    oblocks = cells // ocean_cells
    spread = 2 * REACH + 1
    comp_index = lax.axis_index("comp")
    comp_count = lax.axis_size("comp")
    is_atmos = comp_index < comp_count - 1
    group = jnp.where(is_atmos, 0, 1).astype(jnp.int32)
    rates = lax.dynamic_index_in_dim(mixing, group, 0, keepdims=False)[:, :, None]
    operator = lax.dynamic_index_in_dim(vertical, group, 0, keepdims=False)
    for sweep in range(SUB):
        padded = extended(fields, (("tile", 2),), 1)
        fields = fields + rates * (padded[:, :, :-2] + padded[:, :, 2:] - 2.0 * fields)
    mixed = fields + jnp.einsum("lm,kmz->klz", operator, fields, precision=lax.Precision.HIGHEST)
    surface = jnp.tanh(flux_coef[0][:, None] * mixed[:, -1] + flux_coef[1][:, None] * mixed[:, -2])
    rounded = surface.astype(jnp.bfloat16)
    blocks = rounded.reshape(rounded.shape[0], cells // across, across)
    chosen = blocks[:, atm_block[0, 0], :]
    contrib = jnp.einsum(
        "knb,nbj->nkj", chosen, remap_weights[0, 0], preferred_element_type=jnp.float32
    )
    by_offset = (tile_offset[0, 0][:, None] == jnp.arange(spread, dtype=jnp.int32)[None, :]).astype(
        jnp.float32
    )
    by_block = (ocean_block[0, 0][:, None] == jnp.arange(oblocks, dtype=jnp.int32)[None, :]).astype(
        jnp.float32
    )
    buffers = jnp.einsum(
        "nd,no,nkj->dkoj", by_offset, by_block, contrib, precision=lax.Precision.HIGHEST
    )
    buffers = buffers.reshape(spread, rounded.shape[0], cells)
    buffers = jnp.where(is_atmos, buffers, 0.0)
    received = buffers[REACH]
    for offset in range(-REACH, REACH + 1):
        if offset != 0:
            received = received + passed_along(buffers[REACH + offset], "tile", offset)
    received = lax.psum(received, "comp")
    land = ocean_mask[0].astype(jnp.float32)
    atmosphere = mixed.at[:, -1].add(-0.5 * surface)
    ocean = mixed.at[:, 0].add(land[None, :] * received)
    result = jnp.where(is_atmos, atmosphere, ocean)
    return result[None, None]


def solution(mesh):
    placed = (
        P("comp", "tile", None, None, None),
        P(),
        P(),
        P(),
        P("comp", "tile", None),
        P("comp", "tile", None),
        P("comp", "tile", None),
        P("comp", "tile", None, None, None),
        P("tile", None),
    )
    return jax.shard_map(
        local,
        mesh=mesh,
        in_specs=placed,
        out_specs=P("comp", "tile", None, None, None),
        check_vma=False,
    )
```

profile of v0, /device:TPU:0, one launch (start us, length us, event | category | flops | bytes accessed | tf_op | source)
XLA Modules:
  0.0 47.1 jit_solution(6400851959491823201)
XLA Ops:
  0.0 1.4 %copy.46 = f32[1,1,4,16,2048]{4,2,3,1,0:T(4,128)S(1)} copy(f32[1,1,4,16,2048]{4,3,2,1,0:T(8,128)} %param.13) | data formatting | bytes 1048576 | tf_op args[0]
  1.4 0.1 fusion.36
  1.5 3.0 %collective-permute-start = (f32[4,16,1]{2,0,1:T(4,128)S(1)}, f32[4,16,1]{2,0,1:T(4,128)S(1)}, u32[]{:S(2)}, u32[]{:S(2)}) collective-permute-start(f32[4,16,1]{2,0,1:T(4,128)S(1)} %get-tuple-element.35), channel_id=1, source_target_pairs={{0,1},{1,2},{2,3},{3,4},{4,5},{5,6},{6,7},{7,0},{8,9},{9,10},{10,1... | collective-permute-start | bytes 776 | tf_op jit(solution)/shard_map/ppermute | solution.py:17
  4.5 3.1 %collective-permute-start.1 = (f32[4,16,1]{2,0,1:T(4,128)S(1)}, f32[4,16,1]{2,0,1:T(4,128)S(1)}, u32[]{:S(2)}, u32[]{:S(2)}) collective-permute-start(f32[4,16,1]{2,0,1:T(4,128)S(1)} %get-tuple-element.36), channel_id=1, source_target_pairs={{1,0},{2,1},{3,2},{4,3},{5,4},{6,5},{7,6},{0,7},{9,8},{10,9},{11,1... | collective-permute-start | bytes 776 | tf_op jit(solution)/shard_map/ppermute | solution.py:19
  7.6 0.7 %copy-done.4 = f32[2,4]{1,0:T(2,128)S(1)} copy-done((f32[2,4]{1,0:T(2,128)S(1)}, f32[2,4]{1,0:T(2,128)}, u32[]{:S(2)}) %copy-start.4) | copy-done | bytes 56
  8.3 0.6 %copy-done.7 = s32[1,1,16]{2,1,0:T(1,128)S(1)} copy-done((s32[1,1,16]{2,1,0:T(1,128)S(1)}, s32[1,1,16]{2,1,0:T(1,128)}, u32[]{:S(2)}) %copy-start.7) | copy-done | bytes 88
  9.0 0.7 %copy-done.5 = s32[1,1,16]{2,1,0:T(1,128)S(1)} copy-done((s32[1,1,16]{2,1,0:T(1,128)S(1)}, s32[1,1,16]{2,1,0:T(1,128)}, u32[]{:S(2)}) %copy-start.5) | copy-done | bytes 88
  9.6 0.7 %copy-done.6 = s32[1,1,16]{2,1,0:T(1,128)S(1)} copy-done((s32[1,1,16]{2,1,0:T(1,128)S(1)}, s32[1,1,16]{2,1,0:T(1,128)}, u32[]{:S(2)}) %copy-start.6) | copy-done | bytes 88
  10.3 0.7 %copy-done.3 = f32[2,4,16]{2,1,0:T(4,128)S(1)} copy-done((f32[2,4,16]{2,1,0:T(4,128)S(1)}, f32[2,4,16]{2,1,0:T(4,128)}, u32[]{:S(2)}) %copy-start.3) | copy-done | bytes 536
  11.0 0.1 copy.13
  11.1 0.6 %fusion.8 = f32[4,16,2048]{2,0,1:T(4,128)S(1)} fusion(f32[4,16,2048]{2,0,1:T(4,128)S(1)} %bitcast.114, f32[4,16,1]{2,0,1:T(4,128)S(1)} %collective-permute-done.1, f32[4,16,1]{2,0,1:T(4,128)S(1)} %collective-permute-done, f32[4,16]{0,1:T(8,128)S(1)} %copy.13), kind=kLoop, calls=%fused_computation.13 | loop fusion | flops 917504 | bytes 1049344 | tf_op jit(solution)/shard_map/add | solution.py:57
  11.8 4.7 %collective-permute-start.3 = (f32[4,16,1]{2,0,1:T(4,128)S(1)}, f32[4,16,1]{2,0,1:T(4,128)S(1)}, u32[]{:S(2)}, u32[]{:S(2)}) collective-permute-start(f32[4,16,1]{2,0,1:T(4,128)S(1)} %get-tuple-element.34), channel_id=1, source_target_pairs={{1,0},{2,1},{3,2},{4,3},{5,4},{6,5},{7,6},{0,7},{9,8},{10,9},{11,1... | collective-permute-start | bytes 776 | tf_op jit(solution)/shard_map/ppermute | solution.py:19
  16.5 1.9 %collective-permute-done.2 = f32[4,16,1]{2,0,1:T(4,128)S(1)} collective-permute-done((f32[4,16,1]{2,0,1:T(4,128)S(1)}, f32[4,16,1]{2,0,1:T(4,128)S(1)}, u32[]{:S(2)}, u32[]{:S(2)}) %collective-permute-start.2) | collective-permute-done | bytes 288 | tf_op jit(solution)/shard_map/ppermute | solution.py:17
  18.4 0.6 %fusion.4 = f32[4,16,2048]{2,0,1:T(4,128)S(1)} fusion(f32[4,16,2048]{2,0,1:T(4,128)S(1)} %fusion.8, f32[4,16,1]{2,0,1:T(4,128)S(1)} %collective-permute-done.3, f32[4,16,1]{2,0,1:T(4,128)S(1)} %collective-permute-done.2, f32[4,16]{0,1:T(8,128)S(1)} %copy.13), kind=kLoop, calls=%fused_computation.7 | loop fusion | flops 917504 | bytes 1049344 | tf_op jit(solution)/shard_map/add | solution.py:57
  19.1 0.9 %fusion.11 = f32[4,2048,16]{1,2,0:T(8,128)S(1)} fusion(f32[4,16,2048]{2,0,1:T(4,128)S(1)} %fusion.4, f32[2,16,16]{2,1,0:T(8,128)S(1)} %copy-done.2, s32[]{:T(128)S(6)} %select_n.39), kind=kOutput, calls=%fused_computation.18 | convolution fusion | flops 25165824 | bytes 1056772 | tf_op jit(solution)/shard_map/lm,kmz->klz/dot_general | solution.py:58
  20.0 0.7 %bitcast_add_fusion = f32[4,16,2048]{2,0,1:T(4,128)S(1)} fusion(f32[4,2048,16]{1,2,0:T(8,128)S(1)} %fusion.11, f32[4,16,2048]{2,0,1:T(4,128)S(1)} %fusion.8, f32[4,16,1]{2,0,1:T(4,128)S(1)} %collective-permute-done.3, f32[4,16,1]{2,0,1:T(4,128)S(1)} %collective-permute-done.2, f32[4,16]{0,1:T(8,128)S(1)} %copy.13), kind=kLoop, calls=%fused_computation.17 | loop fusion | flops 1048576 | bytes 1573632 | tf_op jit(solution)/shard_map/add | solution.py:58
  20.7 0.1 fusion.22
  20.8 0.6 %gather_fusion = bf16[16,4,128]{2,1,0:T(4,128)(2,1)S(1)} fusion(bf16[4,16,128]{2,0,1:T(4,128)(2,1)S(1)} %copy.16, s32[1024]{0:T(1024)S(1)} %pad_clamp_fusion), kind=kCustom, calls=%fused_computation | custom fusion | bytes 32832 | tf_op jit(solution)/shard_map/gather | solution.py:62
  21.4 0.2 fusion.9
  21.6 0.3 fusion
  22.0 1.6 %collective-permute-start.4 = (f32[4,2048]{1,0:T(4,128)S(1)}, f32[4,2048]{1,0:T(4,128)S(1)}, u32[]{:S(2)}, u32[]{:S(2)}) collective-permute-start(f32[4,2048]{1,0:T(4,128)S(1)} %bitcast.117), channel_id=1, source_target_pairs={{0,5},{1,6},{2,7},{3,0},{4,1},{5,2},{6,3},{7,4},{8,13},{9,14},{10,... | collective-permute-start | bytes 98312 | tf_op jit(solution)/shard_map/ppermute | solution.py:29
  23.7 1.4 %collective-permute-start.5 = (f32[4,2048]{1,0:T(4,128)S(1)}, f32[4,2048]{1,0:T(4,128)S(1)}, u32[]{:S(2)}, u32[]{:S(2)}) collective-permute-start(f32[4,2048]{1,0:T(4,128)S(1)} %bitcast.115), channel_id=1, source_target_pairs={{0,6},{1,7},{2,0},{3,1},{4,2},{5,3},{6,4},{7,5},{8,14},{9,15},{10,... | collective-permute-start | bytes 98312 | tf_op jit(solution)/shard_map/ppermute | solution.py:29
  25.1 1.9 %collective-permute-start.6 = (f32[4,2048]{1,0:T(4,128)S(1)}, f32[4,2048]{1,0:T(4,128)S(1)}, u32[]{:S(2)}, u32[]{:S(2)}) collective-permute-start(f32[4,2048]{1,0:T(4,128)S(1)} %bitcast.116), channel_id=1, source_target_pairs={{0,7},{1,0},{2,1},{3,2},{4,3},{5,4},{6,5},{7,6},{8,15},{9,8},{10,9... | collective-permute-start | bytes 98312 | tf_op jit(solution)/shard_map/ppermute | solution.py:29
  27.0 0.6 %collective-permute-start.7 = (f32[4,2048]{1,0:T(4,128)S(1)}, f32[4,2048]{1,0:T(4,128)S(1)}, u32[]{:S(2)}, u32[]{:S(2)}) collective-permute-start(f32[4,2048]{1,0:T(4,128)S(1)} %bitcast.118), channel_id=1, source_target_pairs={{0,1},{1,2},{2,3},{3,4},{4,5},{5,6},{6,7},{7,0},{8,9},{9,10},{10,1... | collective-permute-start | bytes 98312 | tf_op jit(solution)/shard_map/ppermute | solution.py:29
  27.6 2.1 %collective-permute-start.8 = (f32[4,2048]{1,0:T(4,128)S(1)}, f32[4,2048]{1,0:T(4,128)S(1)}, u32[]{:S(2)}, u32[]{:S(2)}) collective-permute-start(f32[4,2048]{1,0:T(4,128)S(1)} %bitcast.119), channel_id=1, source_target_pairs={{0,2},{1,3},{2,4},{3,5},{4,6},{5,7},{6,0},{7,1},{8,10},{9,11},{10,... | collective-permute-start | bytes 98312 | tf_op jit(solution)/shard_map/ppermute | solution.py:29
  29.7 1.5 %collective-permute-start.9 = (f32[4,2048]{1,0:T(4,128)S(1)}, f32[4,2048]{1,0:T(4,128)S(1)}, u32[]{:S(2)}, u32[]{:S(2)}) collective-permute-start(f32[4,2048]{1,0:T(4,128)S(1)} %bitcast.120), channel_id=1, source_target_pairs={{0,3},{1,4},{2,5},{3,6},{4,7},{5,0},{6,1},{7,2},{8,11},{9,12},{10,... | collective-permute-start | bytes 98312 | tf_op jit(solution)/shard_map/ppermute | solution.py:29
  31.3 2.3 %collective-permute-done.7 = f32[4,2048]{1,0:T(4,128)S(1)} collective-permute-done((f32[4,2048]{1,0:T(4,128)S(1)}, f32[4,2048]{1,0:T(4,128)S(1)}, u32[]{:S(2)}, u32[]{:S(2)}) %collective-permute-start.7) | collective-permute-done | bytes 32800 | tf_op jit(solution)/shard_map/ppermute | solution.py:29
  33.6 1.8 %collective-permute-done.9 = f32[4,2048]{1,0:T(4,128)S(1)} collective-permute-done((f32[4,2048]{1,0:T(4,128)S(1)}, f32[4,2048]{1,0:T(4,128)S(1)}, u32[]{:S(2)}, u32[]{:S(2)}) %collective-permute-start.9) | collective-permute-done | bytes 32800 | tf_op jit(solution)/shard_map/ppermute | solution.py:29
  35.5 10.3 %psum.7 = f32[4,2048]{1,0:T(4,128)S(1)} all-reduce(f32[4,2048]{1,0:T(4,128)S(1)} %fusion.19), channel_id=1, replica_groups=mesh['comp'=4,'tile'=8] {'comp'}, use_global_device_ids=true, to_apply=%region_0.1 | all-reduce | flops 8192 | bytes 65536 | tf_op jit(solution)/shard_map/psum | solution.py:81
  45.8 0.1 add_dynamic-update-slice_fusion
  45.9 0.1 select_bitcast_fusion
  46.0 1.1 %copy.18 = f32[1,1,4,16,2048]{4,3,2,1,0:T(8,128)} copy(f32[1,1,4,16,2048]{4,2,3,1,0:T(4,128)S(1)} %select_bitcast_fusion) | data formatting | bytes 1048576 | tf_op jit(solution)/shard_map/broadcast_in_dim | solution.py:86
  (39 shorter events, 0.4 us)
Async XLA Ops:
  0.0 21.4 %copy-start = (bf16[1,1,16,128,128]{4,3,2,1,0:T(8,128)(2,1)S(1)}, bf16[1,1,16,128,128]{4,3,2,1,0:T(8,128)(2,1)}, u32[]{:S(2)}) copy-start(bf16[1,1,16,128,128]{4,3,2,1,0:T(8,128)(2,1)} %param.20) | copy-start | bytes 1572868
  1.5 9.5 %collective-permute-start = (f32[4,16,1]{2,0,1:T(4,128)S(1)}, f32[4,16,1]{2,0,1:T(4,128)S(1)}, u32[]{:S(2)}, u32[]{:S(2)}) collective-permute-start(f32[4,16,1]{2,0,1:T(4,128)S(1)} %get-tuple-element.35), channel_id=1, source_target_pairs={{0,1},{1,2},{2,3},{3,4},{4,5},{5,6},{6,7},{7,0},{8,9},{9,10},{10,1... | collective-permute-start | bytes 776 | tf_op jit(solution)/shard_map/ppermute | solution.py:17
  4.5 6.5 %collective-permute-start.1 = (f32[4,16,1]{2,0,1:T(4,128)S(1)}, f32[4,16,1]{2,0,1:T(4,128)S(1)}, u32[]{:S(2)}, u32[]{:S(2)}) collective-permute-start(f32[4,16,1]{2,0,1:T(4,128)S(1)} %get-tuple-element.36), channel_id=1, source_target_pairs={{1,0},{2,1},{3,2},{4,3},{5,4},{6,5},{7,6},{0,7},{9,8},{10,9},{11,1... | collective-permute-start | bytes 776 | tf_op jit(solution)/shard_map/ppermute | solution.py:19
  7.6 0.7 %copy-start.4 = (f32[2,4]{1,0:T(2,128)S(1)}, f32[2,4]{1,0:T(2,128)}, u32[]{:S(2)}) copy-start(f32[2,4]{1,0:T(2,128)} %param.16) | copy-start | bytes 100
  8.3 0.7 %copy-start.7 = (s32[1,1,16]{2,1,0:T(1,128)S(1)}, s32[1,1,16]{2,1,0:T(1,128)}, u32[]{:S(2)}) copy-start(s32[1,1,16]{2,1,0:T(1,128)} %param.17) | copy-start | bytes 196
  9.0 0.7 %copy-start.5 = (s32[1,1,16]{2,1,0:T(1,128)S(1)}, s32[1,1,16]{2,1,0:T(1,128)}, u32[]{:S(2)}) copy-start(s32[1,1,16]{2,1,0:T(1,128)} %param.18) | copy-start | bytes 196
  9.6 0.7 %copy-start.6 = (s32[1,1,16]{2,1,0:T(1,128)S(1)}, s32[1,1,16]{2,1,0:T(1,128)}, u32[]{:S(2)}) copy-start(s32[1,1,16]{2,1,0:T(1,128)} %param.19) | copy-start | bytes 196
  10.3 0.7 %copy-start.3 = (f32[2,4,16]{2,1,0:T(4,128)S(1)}, f32[2,4,16]{2,1,0:T(4,128)}, u32[]{:S(2)}) copy-start(f32[2,4,16]{2,1,0:T(4,128)} %param.14) | copy-start | bytes 1540
  11.8 6.6 %collective-permute-start.2 = (f32[4,16,1]{2,0,1:T(4,128)S(1)}, f32[4,16,1]{2,0,1:T(4,128)S(1)}, u32[]{:S(2)}, u32[]{:S(2)}) collective-permute-start(f32[4,16,1]{2,0,1:T(4,128)S(1)} %get-tuple-element.33), channel_id=1, source_target_pairs={{0,1},{1,2},{2,3},{3,4},{4,5},{5,6},{6,7},{7,0},{8,9},{9,10},{10,1... | collective-permute-start | bytes 776 | tf_op jit(solution)/shard_map/ppermute | solution.py:17
  11.8 6.6 %collective-permute-start.3 = (f32[4,16,1]{2,0,1:T(4,128)S(1)}, f32[4,16,1]{2,0,1:T(4,128)S(1)}, u32[]{:S(2)}, u32[]{:S(2)}) collective-permute-start(f32[4,16,1]{2,0,1:T(4,128)S(1)} %get-tuple-element.34), channel_id=1, source_target_pairs={{1,0},{2,1},{3,2},{4,3},{5,4},{6,5},{7,6},{0,7},{9,8},{10,9},{11,1... | collective-permute-start | bytes 776 | tf_op jit(solution)/shard_map/ppermute | solution.py:19
  16.5 2.5 %copy-start.2 = (f32[2,16,16]{2,1,0:T(8,128)S(1)}, f32[2,16,16]{2,1,0:T(8,128)}, u32[]{:S(2)}) copy-start(f32[2,16,16]{2,1,0:T(8,128)} %param.15) | copy-start | bytes 6148
  22.0 7.7 %collective-permute-start.4 = (f32[4,2048]{1,0:T(4,128)S(1)}, f32[4,2048]{1,0:T(4,128)S(1)}, u32[]{:S(2)}, u32[]{:S(2)}) collective-permute-start(f32[4,2048]{1,0:T(4,128)S(1)} %bitcast.117), channel_id=1, source_target_pairs={{0,5},{1,6},{2,7},{3,0},{4,1},{5,2},{6,3},{7,4},{8,13},{9,14},{10,... | collective-permute-start | bytes 98312 | tf_op jit(solution)/shard_map/ppermute | solution.py:29
  23.7 7.6 %collective-permute-start.5 = (f32[4,2048]{1,0:T(4,128)S(1)}, f32[4,2048]{1,0:T(4,128)S(1)}, u32[]{:S(2)}, u32[]{:S(2)}) collective-permute-start(f32[4,2048]{1,0:T(4,128)S(1)} %bitcast.115), channel_id=1, source_target_pairs={{0,6},{1,7},{2,0},{3,1},{4,2},{5,3},{6,4},{7,5},{8,14},{9,15},{10,... | collective-permute-start | bytes 98312 | tf_op jit(solution)/shard_map/ppermute | solution.py:29
  25.1 6.2 %collective-permute-start.6 = (f32[4,2048]{1,0:T(4,128)S(1)}, f32[4,2048]{1,0:T(4,128)S(1)}, u32[]{:S(2)}, u32[]{:S(2)}) collective-permute-start(f32[4,2048]{1,0:T(4,128)S(1)} %bitcast.116), channel_id=1, source_target_pairs={{0,7},{1,0},{2,1},{3,2},{4,3},{5,4},{6,5},{7,6},{8,15},{9,8},{10,9... | collective-permute-start | bytes 98312 | tf_op jit(solution)/shard_map/ppermute | solution.py:29
  27.0 6.7 %collective-permute-start.7 = (f32[4,2048]{1,0:T(4,128)S(1)}, f32[4,2048]{1,0:T(4,128)S(1)}, u32[]{:S(2)}, u32[]{:S(2)}) collective-permute-start(f32[4,2048]{1,0:T(4,128)S(1)} %bitcast.118), channel_id=1, source_target_pairs={{0,1},{1,2},{2,3},{3,4},{4,5},{5,6},{6,7},{7,0},{8,9},{9,10},{10,1... | collective-permute-start | bytes 98312 | tf_op jit(solution)/shard_map/ppermute | solution.py:29
  27.6 6.0 %collective-permute-start.8 = (f32[4,2048]{1,0:T(4,128)S(1)}, f32[4,2048]{1,0:T(4,128)S(1)}, u32[]{:S(2)}, u32[]{:S(2)}) collective-permute-start(f32[4,2048]{1,0:T(4,128)S(1)} %bitcast.119), channel_id=1, source_target_pairs={{0,2},{1,3},{2,4},{3,5},{4,6},{5,7},{6,0},{7,1},{8,10},{9,11},{10,... | collective-permute-start | bytes 98312 | tf_op jit(solution)/shard_map/ppermute | solution.py:29
  29.6 1.5 %copy-start.1 = (s32[1,2048]{1,0:T(1,128)S(1)}, s32[1,2048]{1,0:T(1,128)}, u32[]{:S(2)}) copy-start(s32[1,2048]{1,0:T(1,128)} %param.21) | copy-start | bytes 24580
  29.7 5.8 %collective-permute-start.9 = (f32[4,2048]{1,0:T(4,128)S(1)}, f32[4,2048]{1,0:T(4,128)S(1)}, u32[]{:S(2)}, u32[]{:S(2)}) collective-permute-start(f32[4,2048]{1,0:T(4,128)S(1)} %bitcast.120), channel_id=1, source_target_pairs={{0,3},{1,4},{2,5},{3,6},{4,7},{5,0},{6,1},{7,2},{8,11},{9,12},{10,... | collective-permute-start | bytes 98312 | tf_op jit(solution)/shard_map/ppermute | solution.py:29
where the time goes:
time: 47.4 us; the launch traced here: 47.1 us
  starting transfers between devices  19.9 us (42%)
  blocking collectives  10.3 us (22%)
  local copies, waits for them, and re-layouts  6.88 us (15%)
  waiting for transfers between devices  6.07 us (13%)
  other arithmetic  2.36 us (5%)
  matrix products  1.45 us (3%)
    psum x1, blocking collectives, local(): received = lax.psum(received, 'comp')  10.3 us
    ppermute x6, starting transfers between devices, passed_along(): return lax.ppermute(value, axis, pairs)  9.11 us
    ppermute x2, starting transfers between devices, extended(): lax.ppermute(head, axis, [((i + 1) % count, i) for i in range(count)])  7.81 us
    unnamed x26, local copies, waits for them, and re-layouts  4.92 us
    ppermute x6, waiting for transfers between devices, passed_along(): return lax.ppermute(value, axis, pairs)  4.18 us
    ppermute x2, starting transfers between devices, extended(): lax.ppermute(tail, axis, [(i, (i + 1) % count) for i in range(count)])  3.02 us
    ppermute x2, waiting for transfers between devices, extended(): lax.ppermute(tail, axis, [(i, (i + 1) % count) for i in range(count)])  1.88 us
    add x2, other arithmetic, local(): fields + rates * (padded[:, :, :-2] + padded[:, :, 2:] - 2.0 * fields)  1.28 us
  transfers between devices with their start and end apart: 10, of which 3 were waited for; matrix products, arithmetic and copies ran while one was open for 0% of the time, Pallas kernels for 0%

commit v1 on v0

--- a/solution.py
+++ b/solution.py
@@ -78,7 +78,9 @@
     for offset in range(-REACH, REACH + 1):
         if offset != 0:
             received = received + passed_along(buffers[REACH + offset], "tile", offset)
-    received = lax.psum(received, "comp")
+    received = received
+    for hop in (1, 2):
+        received = received + lax.ppermute(received, "comp", [(dev, dev ^ hop) for dev in range(4)])
     land = ocean_mask[0].astype(jnp.float32)
     atmosphere = mixed.at[:, -1].add(-0.5 * surface)
     ocean = mixed.at[:, 0].add(land[None, :] * received)

time: 47.4 us -> 42.4 us (0.89)
  blocking collectives: 10.3 us -> 0 us
  waiting for transfers between devices: 6.07 us -> 9.55 us
  starting transfers between devices: 19.9 us -> 21.7 us
    psum x1 -> x0, blocking collectives: 10.3 us -> none  [local(): received = lax.psum(received, 'comp')]
    ppermute x0 -> x2, waiting for transfers between devices: none -> 3.4 us  [local(): lax.ppermute(received, 'comp', [(dev, dev ^ hop) for dev in range(4)])]
    ppermute x0 -> x2, starting transfers between devices: none -> 1.78 us  [local(): lax.ppermute(received, 'comp', [(dev, dev ^ hop) for dev in range(4)])]
  transfers between devices with their start and end apart: 10 -> 12, of which waited for: 3 -> 5; matrix products, arithmetic and copies ran while one was open for 0% -> 1% of each run, Pallas kernels for 0% -> 0%
where the time goes in v1:
time: 42.4 us; the launch traced here: 42.1 us
  starting transfers between devices  21.7 us (51%)
  waiting for transfers between devices  9.55 us (23%)
  local copies, waits for them, and re-layouts  6.88 us (16%)
  other arithmetic  2.37 us (6%)
  matrix products  1.45 us (3%)
    ppermute x6, starting transfers between devices, passed_along(): return lax.ppermute(value, axis, pairs)  9.11 us
    ppermute x2, starting transfers between devices, extended(): lax.ppermute(head, axis, [((i + 1) % count, i) for i in range(count)])  7.81 us
    unnamed x26, local copies, waits for them, and re-layouts  4.92 us
    ppermute x6, waiting for transfers between devices, passed_along(): return lax.ppermute(value, axis, pairs)  4.26 us
    ppermute x2, waiting for transfers between devices, local(): lax.ppermute(received, 'comp', [(dev, dev ^ hop) for dev in range(4)])  3.4 us
    ppermute x2, starting transfers between devices, extended(): lax.ppermute(tail, axis, [(i, (i + 1) % count) for i in range(count)])  3.02 us
    ppermute x2, waiting for transfers between devices, extended(): lax.ppermute(tail, axis, [(i, (i + 1) % count) for i in range(count)])  1.88 us
    ppermute x2, starting transfers between devices, local(): lax.ppermute(received, 'comp', [(dev, dev ^ hop) for dev in range(4)])  1.78 us
  transfers between devices with their start and end apart: 12, of which 5 were waited for; matrix products, arithmetic and copies ran while one was open for 1% of the time, Pallas kernels for 0%

profile of v1, /device:TPU:0, one launch (start us, length us, event | category | flops | bytes accessed | tf_op | source)
XLA Modules:
  0.0 42.1 jit_solution(11763132214596937610)
XLA Ops:
  0.0 1.4 %copy.46 = f32[1,1,4,16,2048]{4,2,3,1,0:T(4,128)S(1)} copy(f32[1,1,4,16,2048]{4,3,2,1,0:T(8,128)} %param.13) | data formatting | bytes 1048576 | tf_op args[0]
  1.5 3.0 %collective-permute-start = (f32[4,16,1]{2,0,1:T(4,128)S(1)}, f32[4,16,1]{2,0,1:T(4,128)S(1)}, u32[]{:S(2)}, u32[]{:S(2)}) collective-permute-start(f32[4,16,1]{2,0,1:T(4,128)S(1)} %get-tuple-element.35), channel_id=1, source_target_pairs={{0,1},{1,2},{2,3},{3,4},{4,5},{5,6},{6,7},{7,0},{8,9},{9,10},{10,1... | collective-permute-start | bytes 776 | tf_op jit(solution)/shard_map/ppermute | solution.py:17
  4.5 3.1 %collective-permute-start.1 = (f32[4,16,1]{2,0,1:T(4,128)S(1)}, f32[4,16,1]{2,0,1:T(4,128)S(1)}, u32[]{:S(2)}, u32[]{:S(2)}) collective-permute-start(f32[4,16,1]{2,0,1:T(4,128)S(1)} %get-tuple-element.36), channel_id=1, source_target_pairs={{1,0},{2,1},{3,2},{4,3},{5,4},{6,5},{7,6},{0,7},{9,8},{10,9},{11,1... | collective-permute-start | bytes 776 | tf_op jit(solution)/shard_map/ppermute | solution.py:19
  7.6 0.7 %copy-done.4 = f32[2,4]{1,0:T(2,128)S(1)} copy-done((f32[2,4]{1,0:T(2,128)S(1)}, f32[2,4]{1,0:T(2,128)}, u32[]{:S(2)}) %copy-start.4) | copy-done | bytes 56
  8.3 0.6 %copy-done.7 = s32[1,1,16]{2,1,0:T(1,128)S(1)} copy-done((s32[1,1,16]{2,1,0:T(1,128)S(1)}, s32[1,1,16]{2,1,0:T(1,128)}, u32[]{:S(2)}) %copy-start.7) | copy-done | bytes 88
  9.0 0.7 %copy-done.5 = s32[1,1,16]{2,1,0:T(1,128)S(1)} copy-done((s32[1,1,16]{2,1,0:T(1,128)S(1)}, s32[1,1,16]{2,1,0:T(1,128)}, u32[]{:S(2)}) %copy-start.5) | copy-done | bytes 88
  9.6 0.7 %copy-done.6 = s32[1,1,16]{2,1,0:T(1,128)S(1)} copy-done((s32[1,1,16]{2,1,0:T(1,128)S(1)}, s32[1,1,16]{2,1,0:T(1,128)}, u32[]{:S(2)}) %copy-start.6) | copy-done | bytes 88
  10.3 0.7 %copy-done.3 = f32[2,4,16]{2,1,0:T(4,128)S(1)} copy-done((f32[2,4,16]{2,1,0:T(4,128)S(1)}, f32[2,4,16]{2,1,0:T(4,128)}, u32[]{:S(2)}) %copy-start.3) | copy-done | bytes 536
  11.0 0.1 copy.13
  11.1 0.6 %fusion.8 = f32[4,16,2048]{2,0,1:T(4,128)S(1)} fusion(f32[4,16,2048]{2,0,1:T(4,128)S(1)} %bitcast.114, f32[4,16,1]{2,0,1:T(4,128)S(1)} %collective-permute-done.1, f32[4,16,1]{2,0,1:T(4,128)S(1)} %collective-permute-done, f32[4,16]{0,1:T(8,128)S(1)} %copy.13), kind=kLoop, calls=%fused_computation.13 | loop fusion | flops 917504 | bytes 1049344 | tf_op jit(solution)/shard_map/add | solution.py:57
  11.8 4.7 %collective-permute-start.3 = (f32[4,16,1]{2,0,1:T(4,128)S(1)}, f32[4,16,1]{2,0,1:T(4,128)S(1)}, u32[]{:S(2)}, u32[]{:S(2)}) collective-permute-start(f32[4,16,1]{2,0,1:T(4,128)S(1)} %get-tuple-element.34), channel_id=1, source_target_pairs={{1,0},{2,1},{3,2},{4,3},{5,4},{6,5},{7,6},{0,7},{9,8},{10,9},{11,1... | collective-permute-start | bytes 776 | tf_op jit(solution)/shard_map/ppermute | solution.py:19
  16.5 1.9 %collective-permute-done.2 = f32[4,16,1]{2,0,1:T(4,128)S(1)} collective-permute-done((f32[4,16,1]{2,0,1:T(4,128)S(1)}, f32[4,16,1]{2,0,1:T(4,128)S(1)}, u32[]{:S(2)}, u32[]{:S(2)}) %collective-permute-start.2) | collective-permute-done | bytes 288 | tf_op jit(solution)/shard_map/ppermute | solution.py:17
  18.4 0.6 %fusion.4 = f32[4,16,2048]{2,0,1:T(4,128)S(1)} fusion(f32[4,16,2048]{2,0,1:T(4,128)S(1)} %fusion.8, f32[4,16,1]{2,0,1:T(4,128)S(1)} %collective-permute-done.3, f32[4,16,1]{2,0,1:T(4,128)S(1)} %collective-permute-done.2, f32[4,16]{0,1:T(8,128)S(1)} %copy.13), kind=kLoop, calls=%fused_computation.7 | loop fusion | flops 917504 | bytes 1049344 | tf_op jit(solution)/shard_map/add | solution.py:57
  19.1 0.9 %fusion.11 = f32[4,2048,16]{1,2,0:T(8,128)S(1)} fusion(f32[4,16,2048]{2,0,1:T(4,128)S(1)} %fusion.4, f32[2,16,16]{2,1,0:T(8,128)S(1)} %copy-done.2, s32[]{:T(128)S(6)} %select_n.39), kind=kOutput, calls=%fused_computation.18 | convolution fusion | flops 25165824 | bytes 1056772 | tf_op jit(solution)/shard_map/lm,kmz->klz/dot_general | solution.py:58
  20.0 0.7 %bitcast_add_fusion = f32[4,16,2048]{2,0,1:T(4,128)S(1)} fusion(f32[4,2048,16]{1,2,0:T(8,128)S(1)} %fusion.11, f32[4,16,2048]{2,0,1:T(4,128)S(1)} %fusion.8, f32[4,16,1]{2,0,1:T(4,128)S(1)} %collective-permute-done.3, f32[4,16,1]{2,0,1:T(4,128)S(1)} %collective-permute-done.2, f32[4,16]{0,1:T(8,128)S(1)} %copy.13), kind=kLoop, calls=%fused_computation.17 | loop fusion | flops 1048576 | bytes 1573632 | tf_op jit(solution)/shard_map/add | solution.py:58
  20.8 0.6 %gather_fusion = bf16[16,4,128]{2,1,0:T(4,128)(2,1)S(1)} fusion(bf16[4,16,128]{2,0,1:T(4,128)(2,1)S(1)} %copy.16, s32[1024]{0:T(1024)S(1)} %pad_clamp_fusion), kind=kCustom, calls=%fused_computation | custom fusion | bytes 32832 | tf_op jit(solution)/shard_map/gather | solution.py:62
  21.4 0.2 fusion.9
  21.6 0.3 fusion
  22.0 1.6 %collective-permute-start.4 = (f32[4,2048]{1,0:T(4,128)S(1)}, f32[4,2048]{1,0:T(4,128)S(1)}, u32[]{:S(2)}, u32[]{:S(2)}) collective-permute-start(f32[4,2048]{1,0:T(4,128)S(1)} %bitcast.117), channel_id=1, source_target_pairs={{0,5},{1,6},{2,7},{3,0},{4,1},{5,2},{6,3},{7,4},{8,13},{9,14},{10,... | collective-permute-start | bytes 98312 | tf_op jit(solution)/shard_map/ppermute | solution.py:29
  23.7 1.4 %collective-permute-start.5 = (f32[4,2048]{1,0:T(4,128)S(1)}, f32[4,2048]{1,0:T(4,128)S(1)}, u32[]{:S(2)}, u32[]{:S(2)}) collective-permute-start(f32[4,2048]{1,0:T(4,128)S(1)} %bitcast.116), channel_id=1, source_target_pairs={{0,6},{1,7},{2,0},{3,1},{4,2},{5,3},{6,4},{7,5},{8,14},{9,15},{10,... | collective-permute-start | bytes 98312 | tf_op jit(solution)/shard_map/ppermute | solution.py:29
  25.1 1.9 %collective-permute-start.6 = (f32[4,2048]{1,0:T(4,128)S(1)}, f32[4,2048]{1,0:T(4,128)S(1)}, u32[]{:S(2)}, u32[]{:S(2)}) collective-permute-start(f32[4,2048]{1,0:T(4,128)S(1)} %bitcast.118), channel_id=1, source_target_pairs={{0,7},{1,0},{2,1},{3,2},{4,3},{5,4},{6,5},{7,6},{8,15},{9,8},{10,9... | collective-permute-start | bytes 98312 | tf_op jit(solution)/shard_map/ppermute | solution.py:29
  27.0 0.6 %collective-permute-start.7 = (f32[4,2048]{1,0:T(4,128)S(1)}, f32[4,2048]{1,0:T(4,128)S(1)}, u32[]{:S(2)}, u32[]{:S(2)}) collective-permute-start(f32[4,2048]{1,0:T(4,128)S(1)} %bitcast.119), channel_id=1, source_target_pairs={{0,1},{1,2},{2,3},{3,4},{4,5},{5,6},{6,7},{7,0},{8,9},{9,10},{10,1... | collective-permute-start | bytes 98312 | tf_op jit(solution)/shard_map/ppermute | solution.py:29
  27.6 2.1 %collective-permute-start.8 = (f32[4,2048]{1,0:T(4,128)S(1)}, f32[4,2048]{1,0:T(4,128)S(1)}, u32[]{:S(2)}, u32[]{:S(2)}) collective-permute-start(f32[4,2048]{1,0:T(4,128)S(1)} %bitcast.120), channel_id=1, source_target_pairs={{0,2},{1,3},{2,4},{3,5},{4,6},{5,7},{6,0},{7,1},{8,10},{9,11},{10,... | collective-permute-start | bytes 98312 | tf_op jit(solution)/shard_map/ppermute | solution.py:29
  29.7 1.5 %collective-permute-start.9 = (f32[4,2048]{1,0:T(4,128)S(1)}, f32[4,2048]{1,0:T(4,128)S(1)}, u32[]{:S(2)}, u32[]{:S(2)}) collective-permute-start(f32[4,2048]{1,0:T(4,128)S(1)} %bitcast.121), channel_id=1, source_target_pairs={{0,3},{1,4},{2,5},{3,6},{4,7},{5,0},{6,1},{7,2},{8,11},{9,12},{10,... | collective-permute-start | bytes 98312 | tf_op jit(solution)/shard_map/ppermute | solution.py:29
  31.2 2.4 %collective-permute-done.7 = f32[4,2048]{1,0:T(4,128)S(1)} collective-permute-done((f32[4,2048]{1,0:T(4,128)S(1)}, f32[4,2048]{1,0:T(4,128)S(1)}, u32[]{:S(2)}, u32[]{:S(2)}) %collective-permute-start.7) | collective-permute-done | bytes 32800 | tf_op jit(solution)/shard_map/ppermute | solution.py:29
  33.6 1.8 %collective-permute-done.9 = f32[4,2048]{1,0:T(4,128)S(1)} collective-permute-done((f32[4,2048]{1,0:T(4,128)S(1)}, f32[4,2048]{1,0:T(4,128)S(1)}, u32[]{:S(2)}, u32[]{:S(2)}) %collective-permute-start.9) | collective-permute-done | bytes 32800 | tf_op jit(solution)/shard_map/ppermute | solution.py:29
  35.6 1.2 %collective-permute-done.10 = f32[4,2048]{1,0:T(4,128)S(1)} collective-permute-done((f32[4,2048]{1,0:T(4,128)S(1)}, f32[4,2048]{1,0:T(4,128)S(1)}, u32[]{:S(2)}, u32[]{:S(2)}) %collective-permute-start.10) | collective-permute-done | bytes 32800 | tf_op jit(solution)/shard_map/ppermute | solution.py:83
  36.8 1.7 %collective-permute-start.11 = (f32[4,2048]{1,0:T(4,128)S(1)}, f32[4,2048]{1,0:T(4,128)S(1)}, u32[]{:S(2)}, u32[]{:S(2)}) collective-permute-start(f32[4,2048]{1,0:T(4,128)S(1)} %add.89), channel_id=1, source_target_pairs={{0,16},{8,24},{16,0},{24,8},{1,17},{9,25},{17,1},{25,9},{2,18},{10... | collective-permute-start | bytes 98312 | tf_op jit(solution)/shard_map/ppermute | solution.py:83
  38.6 2.2 %collective-permute-done.11 = f32[4,2048]{1,0:T(4,128)S(1)} collective-permute-done((f32[4,2048]{1,0:T(4,128)S(1)}, f32[4,2048]{1,0:T(4,128)S(1)}, u32[]{:S(2)}, u32[]{:S(2)}) %collective-permute-start.11) | collective-permute-done | bytes 32800 | tf_op jit(solution)/shard_map/ppermute | solution.py:83
  40.8 0.1 add_dynamic-update-slice_fusion
  40.9 0.1 select_bitcast_fusion
  41.0 1.1 %copy.18 = f32[1,1,4,16,2048]{4,3,2,1,0:T(8,128)} copy(f32[1,1,4,16,2048]{4,2,3,1,0:T(4,128)S(1)} %select_bitcast_fusion) | data formatting | bytes 1048576 | tf_op jit(solution)/shard_map/broadcast_in_dim | solution.py:88
  (43 shorter events, 0.7 us)
Async XLA Ops:
  0.0 21.4 %copy-start = (bf16[1,1,16,128,128]{4,3,2,1,0:T(8,128)(2,1)S(1)}, bf16[1,1,16,128,128]{4,3,2,1,0:T(8,128)(2,1)}, u32[]{:S(2)}) copy-start(bf16[1,1,16,128,128]{4,3,2,1,0:T(8,128)(2,1)} %param.20) | copy-start | bytes 1572868
  1.5 9.5 %collective-permute-start = (f32[4,16,1]{2,0,1:T(4,128)S(1)}, f32[4,16,1]{2,0,1:T(4,128)S(1)}, u32[]{:S(2)}, u32[]{:S(2)}) collective-permute-start(f32[4,16,1]{2,0,1:T(4,128)S(1)} %get-tuple-element.35), channel_id=1, source_target_pairs={{0,1},{1,2},{2,3},{3,4},{4,5},{5,6},{6,7},{7,0},{8,9},{9,10},{10,1... | collective-permute-start | bytes 776 | tf_op jit(solution)/shard_map/ppermute | solution.py:17
  4.5 6.5 %collective-permute-start.1 = (f32[4,16,1]{2,0,1:T(4,128)S(1)}, f32[4,16,1]{2,0,1:T(4,128)S(1)}, u32[]{:S(2)}, u32[]{:S(2)}) collective-permute-start(f32[4,16,1]{2,0,1:T(4,128)S(1)} %get-tuple-element.36), channel_id=1, source_target_pairs={{1,0},{2,1},{3,2},{4,3},{5,4},{6,5},{7,6},{0,7},{9,8},{10,9},{11,1... | collective-permute-start | bytes 776 | tf_op jit(solution)/shard_map/ppermute | solution.py:19
  7.6 0.7 %copy-start.4 = (f32[2,4]{1,0:T(2,128)S(1)}, f32[2,4]{1,0:T(2,128)}, u32[]{:S(2)}) copy-start(f32[2,4]{1,0:T(2,128)} %param.16) | copy-start | bytes 100
  8.3 0.7 %copy-start.7 = (s32[1,1,16]{2,1,0:T(1,128)S(1)}, s32[1,1,16]{2,1,0:T(1,128)}, u32[]{:S(2)}) copy-start(s32[1,1,16]{2,1,0:T(1,128)} %param.17) | copy-start | bytes 196
  9.0 0.7 %copy-start.5 = (s32[1,1,16]{2,1,0:T(1,128)S(1)}, s32[1,1,16]{2,1,0:T(1,128)}, u32[]{:S(2)}) copy-start(s32[1,1,16]{2,1,0:T(1,128)} %param.18) | copy-start | bytes 196
  9.6 0.7 %copy-start.6 = (s32[1,1,16]{2,1,0:T(1,128)S(1)}, s32[1,1,16]{2,1,0:T(1,128)}, u32[]{:S(2)}) copy-start(s32[1,1,16]{2,1,0:T(1,128)} %param.19) | copy-start | bytes 196
  10.3 0.7 %copy-start.3 = (f32[2,4,16]{2,1,0:T(4,128)S(1)}, f32[2,4,16]{2,1,0:T(4,128)}, u32[]{:S(2)}) copy-start(f32[2,4,16]{2,1,0:T(4,128)} %param.14) | copy-start | bytes 1540
  11.8 6.6 %collective-permute-start.2 = (f32[4,16,1]{2,0,1:T(4,128)S(1)}, f32[4,16,1]{2,0,1:T(4,128)S(1)}, u32[]{:S(2)}, u32[]{:S(2)}) collective-permute-start(f32[4,16,1]{2,0,1:T(4,128)S(1)} %get-tuple-element.33), channel_id=1, source_target_pairs={{0,1},{1,2},{2,3},{3,4},{4,5},{5,6},{6,7},{7,0},{8,9},{9,10},{10,1... | collective-permute-start | bytes 776 | tf_op jit(solution)/shard_map/ppermute | solution.py:17
  11.8 6.6 %collective-permute-start.3 = (f32[4,16,1]{2,0,1:T(4,128)S(1)}, f32[4,16,1]{2,0,1:T(4,128)S(1)}, u32[]{:S(2)}, u32[]{:S(2)}) collective-permute-start(f32[4,16,1]{2,0,1:T(4,128)S(1)} %get-tuple-element.34), channel_id=1, source_target_pairs={{1,0},{2,1},{3,2},{4,3},{5,4},{6,5},{7,6},{0,7},{9,8},{10,9},{11,1... | collective-permute-start | bytes 776 | tf_op jit(solution)/shard_map/ppermute | solution.py:19
  16.5 2.5 %copy-start.2 = (f32[2,16,16]{2,1,0:T(8,128)S(1)}, f32[2,16,16]{2,1,0:T(8,128)}, u32[]{:S(2)}) copy-start(f32[2,16,16]{2,1,0:T(8,128)} %param.15) | copy-start | bytes 6148
  22.0 7.7 %collective-permute-start.4 = (f32[4,2048]{1,0:T(4,128)S(1)}, f32[4,2048]{1,0:T(4,128)S(1)}, u32[]{:S(2)}, u32[]{:S(2)}) collective-permute-start(f32[4,2048]{1,0:T(4,128)S(1)} %bitcast.117), channel_id=1, source_target_pairs={{0,5},{1,6},{2,7},{3,0},{4,1},{5,2},{6,3},{7,4},{8,13},{9,14},{10,... | collective-permute-start | bytes 98312 | tf_op jit(solution)/shard_map/ppermute | solution.py:29
  23.7 7.5 %collective-permute-start.5 = (f32[4,2048]{1,0:T(4,128)S(1)}, f32[4,2048]{1,0:T(4,128)S(1)}, u32[]{:S(2)}, u32[]{:S(2)}) collective-permute-start(f32[4,2048]{1,0:T(4,128)S(1)} %bitcast.116), channel_id=1, source_target_pairs={{0,6},{1,7},{2,0},{3,1},{4,2},{5,3},{6,4},{7,5},{8,14},{9,15},{10,... | collective-permute-start | bytes 98312 | tf_op jit(solution)/shard_map/ppermute | solution.py:29
  25.1 6.1 %collective-permute-start.6 = (f32[4,2048]{1,0:T(4,128)S(1)}, f32[4,2048]{1,0:T(4,128)S(1)}, u32[]{:S(2)}, u32[]{:S(2)}) collective-permute-start(f32[4,2048]{1,0:T(4,128)S(1)} %bitcast.118), channel_id=1, source_target_pairs={{0,7},{1,0},{2,1},{3,2},{4,3},{5,4},{6,5},{7,6},{8,15},{9,8},{10,9... | collective-permute-start | bytes 98312 | tf_op jit(solution)/shard_map/ppermute | solution.py:29
  27.0 6.7 %collective-permute-start.7 = (f32[4,2048]{1,0:T(4,128)S(1)}, f32[4,2048]{1,0:T(4,128)S(1)}, u32[]{:S(2)}, u32[]{:S(2)}) collective-permute-start(f32[4,2048]{1,0:T(4,128)S(1)} %bitcast.119), channel_id=1, source_target_pairs={{0,1},{1,2},{2,3},{3,4},{4,5},{5,6},{6,7},{7,0},{8,9},{9,10},{10,1... | collective-permute-start | bytes 98312 | tf_op jit(solution)/shard_map/ppermute | solution.py:29
  27.6 6.0 %collective-permute-start.8 = (f32[4,2048]{1,0:T(4,128)S(1)}, f32[4,2048]{1,0:T(4,128)S(1)}, u32[]{:S(2)}, u32[]{:S(2)}) collective-permute-start(f32[4,2048]{1,0:T(4,128)S(1)} %bitcast.120), channel_id=1, source_target_pairs={{0,2},{1,3},{2,4},{3,5},{4,6},{5,7},{6,0},{7,1},{8,10},{9,11},{10,... | collective-permute-start | bytes 98312 | tf_op jit(solution)/shard_map/ppermute | solution.py:29
  29.7 5.8 %collective-permute-start.9 = (f32[4,2048]{1,0:T(4,128)S(1)}, f32[4,2048]{1,0:T(4,128)S(1)}, u32[]{:S(2)}, u32[]{:S(2)}) collective-permute-start(f32[4,2048]{1,0:T(4,128)S(1)} %bitcast.121), channel_id=1, source_target_pairs={{0,3},{1,4},{2,5},{3,6},{4,7},{5,0},{6,1},{7,2},{8,11},{9,12},{10,... | collective-permute-start | bytes 98312 | tf_op jit(solution)/shard_map/ppermute | solution.py:29
  35.5 3.0 %copy-start.1 = (s32[1,2048]{1,0:T(1,128)S(1)}, s32[1,2048]{1,0:T(1,128)}, u32[]{:S(2)}) copy-start(s32[1,2048]{1,0:T(1,128)} %param.21) | copy-start | bytes 24580
  35.5 1.3 %collective-permute-start.10 = (f32[4,2048]{1,0:T(4,128)S(1)}, f32[4,2048]{1,0:T(4,128)S(1)}, u32[]{:S(2)}, u32[]{:S(2)}) collective-permute-start(f32[4,2048]{1,0:T(4,128)S(1)} %fusion.19), channel_id=1, source_target_pairs={{0,8},{8,0},{16,24},{24,16},{1,9},{9,1},{17,25},{25,17},{2,10},{10... | collective-permute-start | bytes 98312 | tf_op jit(solution)/shard_map/ppermute | solution.py:83
  36.8 4.0 %collective-permute-start.11 = (f32[4,2048]{1,0:T(4,128)S(1)}, f32[4,2048]{1,0:T(4,128)S(1)}, u32[]{:S(2)}, u32[]{:S(2)}) collective-permute-start(f32[4,2048]{1,0:T(4,128)S(1)} %add.89), channel_id=1, source_target_pairs={{0,16},{8,24},{16,0},{24,8},{1,17},{9,25},{17,1},{25,9},{2,18},{10... | collective-permute-start | bytes 98312 | tf_op jit(solution)/shard_map/ppermute | solution.py:83
